TPU v7x, 256 devices: a whole 4x4x8 slice. The times are simulated.
256 devices in a mesh: row: 32 (over x, z), col: 8 (over y, core).
Axes of the slice: x: 4, y: 4, z: 8, core: 2. Of those that a mesh axis runs over, the one named last changes fastest.
Arguments:
- incident: float32 [2, 36, 32768], P(None, None, 'row'), may hold values from -24 to 24
- diagonal: float32 [32768], P('row'), may hold values from 1 to 2
- near_blocks: bfloat16 [32, 8, 2, 1024, 1024], P('row', None, None, None, 'col'), may hold values from -0.046875 to 0.046875
- left_factors: bfloat16 [32, 32, 2, 64, 1024], P('row', 'col'), may hold values from -0.0390625 to 0.0390625
- right_factors: bfloat16 [32, 32, 2, 64, 1024], P('row', 'col'), may hold values from -0.1875 to 0.1875
- flags: int32 [32, 8], P('row'), may hold values from 0 to 1, as said below
- ranks: int32 [32, 32], P('row', 'col'), may hold values from 4 to 64
- harmonics: float32 [2, 36, 32768], P(None, None, 'row'), may hold values from -0.03125 to 0.03125
Outputs:
- solution: float32 [2, 36, 32768], P(None, None, 'row')
- coefficients: float32 [2, 36, 36], replicated
Inputs may be any that keep to these rules, and one draw needn't show every extreme that they name: `flags`: slot 8 / 2 (the pair of a cluster with itself) is always 1; the ones of a row form one run of slots around it.
All inputs are finite; a program needn't handle non-finite values.
Results may differ from a plain program's by a relative error of at most 0.0013.
Values may be sent and summed in bfloat16 or wider, within the bound.
A program may use at most 128 MiB of HBM per device.

v0:
```python
from functools import partial
import jax
import jax.numpy as jnp
from jax import lax
from jax.sharding import PartitionSpec as P

highest = lax.Precision.HIGHEST


def dense_term(vector, block):

    def product(left, right):
        return jnp.einsum("sf,ef->se", left, right, preferred_element_type=jnp.float32)

    real_out = product(vector[0], block[0]) - product(vector[1], block[1])
    imag_out = product(vector[0], block[1]) + product(vector[1], block[0])
    return jnp.stack([real_out, imag_out])


def lowrank_term(vector, left_block, right_block, rank):

    def inner(left, right):
        return jnp.einsum("sf,rf->sr", left, right, preferred_element_type=jnp.float32)

    def outer(left, right):
        return jnp.einsum("sr,re->se", left, right, preferred_element_type=jnp.float32)

    coeff_real = inner(vector[0], right_block[0]) - inner(vector[1], right_block[1])
    coeff_imag = inner(vector[0], right_block[1]) + inner(vector[1], right_block[0])
    keep = (jnp.arange(right_block.shape[1], dtype=jnp.int32) < rank)[None, None, :]
    coeffs = jnp.where(keep, jnp.stack([coeff_real, coeff_imag]), 0.0).astype(jnp.bfloat16)
    real_out = outer(coeffs[0], left_block[0]) - outer(coeffs[1], left_block[1])
    imag_out = outer(coeffs[0], left_block[1]) + outer(coeffs[1], left_block[0])
    return jnp.stack([real_out, imag_out])


def inner_products(first, second):
    return jnp.einsum("csn,ctn->st", first, second, precision=highest)


def combine_rows(matrix, vectors):
    return jnp.einsum("st,ctn->csn", matrix, vectors, precision=highest)


def matmul(left, right):
    return jnp.dot(left, right, precision=highest)


def lower_inverse(lower):
    identity = jnp.eye(lower.shape[0], dtype=lower.dtype)
    return lax.linalg.triangular_solve(lower, identity, left_side=True, lower=True)


def project(harmonics, vectors):

    def contract(left, right):
        return jnp.einsum("mn,sn->ms", left, right, precision=highest)

    real_out = contract(harmonics[0], vectors[0]) + contract(harmonics[1], vectors[1])
    imag_out = contract(harmonics[0], vectors[1]) - contract(harmonics[1], vectors[0])
    return jnp.stack([real_out, imag_out])


def body(incident, diagonal, near_blocks, left_factors, right_factors, flags, ranks, harmonics):
    blocks = left_factors.shape[1]
    slots = near_blocks.shape[1]
    width = near_blocks.shape[4]
    half_band = slots // 2
    elements = incident.shape[2]
    fields = incident.shape[1]
    clusters = lax.axis_size("row")
    row_index = lax.axis_index("row")
    column = lax.axis_index("col")
    empty = jnp.zeros((2, fields, elements), jnp.float32)

    def far_term(number, piece):
        cluster = column * blocks + number
        offset = (cluster - row_index + half_band) % clusters
        is_near = (offset < slots) & (flags[0, jnp.minimum(offset, slots - 1)] == 1)
        return lax.cond(
            is_near,
            lambda operand: empty,
            partial(
                lowrank_term,
                left_block=left_factors[0, number],
                right_block=right_factors[0, number],
                rank=ranks[0, number],
            ),
            piece,
        )

    def near_term(slot, piece):
        return lax.cond(
            flags[0, slot] == 1,
            partial(dense_term, block=near_blocks[0, slot]),
            lambda operand: empty,
            piece,
        )

    def apply_operator(vector):
        rounded = vector.astype(jnp.bfloat16)
        gathered = lax.all_gather(rounded, "row", axis=2, tiled=True)
        far_pieces = [
            lax.dynamic_slice_in_dim(gathered, (column * blocks + number) * elements, elements, 2)
            for number in range(blocks)
        ]
        near_pieces = [
            lax.dynamic_slice_in_dim(
                gathered,
                (row_index + slot - half_band) % clusters * elements + column * width,
                width,
                2,
            )
            for slot in range(slots)
        ]
        total = near_term(0, near_pieces[0])
        for slot in range(1, slots):
            total = total + near_term(slot, near_pieces[slot])
        for number in range(blocks):
            total = total + far_term(number, far_pieces[number])
        summed = lax.psum(total, "col")
        return summed + diagonal[None, None, :] * vector

    lower_first = jnp.linalg.cholesky(lax.psum(inner_products(incident, incident), "row"))
    basis_one = combine_rows(lower_inverse(lower_first), incident)
    image = apply_operator(basis_one)
    coupling_one = lax.psum(inner_products(image, basis_one), "row")
    rest = image - combine_rows(coupling_one, basis_one)
    gram_one = lax.psum(inner_products(rest, rest), "row")
    lower_second = jnp.linalg.cholesky(gram_one)
    basis_two = combine_rows(lower_inverse(lower_second), rest)
    image = apply_operator(basis_two)
    coupling_onetwo, coupling_two = lax.psum(
        (inner_products(image, basis_one), inner_products(image, basis_two)), "row"
    )
    rest = image - combine_rows(coupling_onetwo, basis_one) - combine_rows(coupling_two, basis_two)
    gram_two = lax.psum(inner_products(rest, rest), "row")
    upper_left = matmul(coupling_one, coupling_one.T) + gram_one
    upper_right = matmul(coupling_one, coupling_onetwo.T) + matmul(lower_second, coupling_two.T)
    lower_right = (
        matmul(coupling_onetwo, coupling_onetwo.T) + matmul(coupling_two, coupling_two.T) + gram_two
    )
    normal = jnp.concatenate(
        [
            jnp.concatenate([upper_left, upper_right], axis=1),
            jnp.concatenate([upper_right.T, lower_right], axis=1),
        ],
        axis=0,
    )
    target = jnp.concatenate(
        [matmul(lower_first, coupling_one.T), matmul(lower_first, coupling_onetwo.T)], axis=1
    )
    factor_inverse = lower_inverse(jnp.linalg.cholesky(normal))
    weights = matmul(factor_inverse.T, matmul(factor_inverse, target.T)).T
    first_weights = weights[:, :fields]
    second_weights = weights[:, fields:]
    solution = combine_rows(first_weights, basis_one) + combine_rows(second_weights, basis_two)
    coefficients = lax.psum(project(harmonics, solution), "row")
    return (solution, coefficients)


def solution(mesh):
    in_specs = (
        P(None, None, "row"),
        P("row"),
        P("row", None, None, None, "col"),
        P("row", "col", None, None, None),
        P("row", "col", None, None, None),
        P("row", None),
        P("row", "col"),
        P(None, None, "row"),
    )
    out_specs = (P(None, None, "row"), P())
    return jax.shard_map(body, mesh=mesh, in_specs=in_specs, out_specs=out_specs, check_vma=False)
```

profile of v0, /device:TPU:0, one launch (start us, length us, event | category | flops | bytes accessed | tf_op | source)
XLA Modules:
  0.0 1355.9 jit_solution(15684794761179191939)
XLA Ops:
  7.2 1.6 convolution_bitcast_fusion.12
  8.8 144.0 %psum.63 = f32[36,36]{0,1:T(8,128)S(1)} all-reduce(f32[36,36]{0,1:T(8,128)S(1)} %convolution_bitcast_fusion.12), channel_id=1, replica_groups=mesh['row'=32,'col'=8] {'row'}, use_global_device_ids=true, to_apply=%region_0.0 | all-reduce | flops 1296 | bytes 10368 | tf_op jit(solution)/shard_map/psum | solution.py:124
  152.9 3.3 cholesky.81
  157.5 2.8 custom-call.13
  160.5 2.1 fusion.542
  163.0 1.8 fusion.540
  172.2 1.5 fusion.541
  173.7 2.8 slice_bitcast_fusion.62
  176.5 1.4 slice_bitcast_fusion.54
  178.0 64.0 %all-gather.3.cloned.1.call-done = bf16[2,36,32768]{2,1,0:T(8,128)(2,1)} async-done(((bf16[2,36,1024]{2,1,0:T(8,128)(2,1)}), bf16[2,36,32768]{2,1,0:T(8,128)(2,1)}) %all-gather.3.cloned.1.call-update) | async-done | bytes 4718608 | tf_op jit(solution)/shard_map/all_gather | solution.py:102
  245.0 6.4 conditional.31
  245.0 1.9 fusion.114
  246.9 1.3 fusion.112
  248.2 1.2 fusion.118
  249.4 1.3 fusion.113
  251.5 6.4 conditional.30
  251.5 1.9 fusion.98
  253.4 1.3 fusion.96
  254.7 1.2 fusion.102
  255.9 1.3 fusion.97
  257.9 4.9 conditional.29
  257.9 1.7 fusion.82
  262.8 4.9 conditional.28
  267.7 4.8 conditional.27
  272.5 4.8 conditional.26
  277.3 4.8 conditional.24
  282.1 4.8 conditional.25
  286.9 3.0 add_add_fusion.1
  290.0 99.7 %all-reduce.4.cloned.1.call-done = f32[2,36,1024]{2,1,0:T(8,128)} async-done(((f32[2,36,1024]{2,1,0:T(8,128)}), f32[2,36,1024]{2,1,0:T(8,128)}) %all-reduce.4.cloned.1.call-update) | async-done | bytes 294928 | tf_op jit(solution)/shard_map/psum | solution.py:121
  389.7 1.4 convolution_bitcast_fusion.10
  391.1 143.1 %psum.65 = f32[36,36]{1,0:T(8,128)S(1)} all-reduce(f32[36,36]{1,0:T(8,128)S(1)} %convolution_bitcast_fusion.10), channel_id=1, replica_groups=mesh['row'=32,'col'=8] {'row'}, use_global_device_ids=true, to_apply=%region_28.31 | all-reduce | flops 1296 | bytes 10368 | tf_op jit(solution)/shard_map/psum | solution.py:127
  534.2 1.4 fusion.491
  536.7 137.9 %psum.66 = f32[36,36]{1,0:T(8,128)S(1)} all-reduce(f32[36,36]{1,0:T(8,128)S(1)} %convolution_bitcast_fusion.9), channel_id=1, replica_groups=mesh['row'=32,'col'=8] {'row'}, use_global_device_ids=true, to_apply=%region_29.32 | all-reduce | flops 1296 | bytes 10368 | tf_op jit(solution)/shard_map/psum | solution.py:129
  674.8 3.3 cholesky.92
  679.5 2.8 custom-call.14
  682.5 2.1 fusion.543
  684.6 2.1 fusion.539
  687.5 73.5 %all-gather.5.cloned.1.call-done = bf16[2,36,32768]{2,1,0:T(8,128)(2,1)} async-done(((bf16[2,36,1024]{2,1,0:T(8,128)(2,1)}), bf16[2,36,32768]{2,1,0:T(8,128)(2,1)}) %all-gather.5.cloned.1.call-update) | async-done | bytes 4718608 | tf_op jit(solution)/shard_map/all_gather | solution.py:102
  764.1 5.7 conditional.43
  765.3 1.3 fusion.356
  767.8 1.3 fusion.357
  769.9 5.7 conditional.42
  771.1 1.3 fusion.340
  772.3 1.2 fusion.346
  773.6 1.3 fusion.341
  775.6 5.7 conditional.41
  776.8 1.3 fusion.324
  778.1 1.2 fusion.330
  779.3 1.3 fusion.325
  781.3 4.0 conditional.40
  786.1 4.8 conditional.39
  790.8 4.9 conditional.38
  795.7 4.1 conditional.36
  799.8 4.1 conditional.37
  803.9 2.5 add_add_fusion
  807.4 97.7 %all-reduce.6.cloned.1.call-done = f32[2,36,1024]{2,1,0:T(8,128)} async-done(((f32[2,36,1024]{2,1,0:T(8,128)}), f32[2,36,1024]{2,1,0:T(8,128)}) %all-reduce.6.cloned.1.call-update) | async-done | bytes 294928 | tf_op jit(solution)/shard_map/psum | solution.py:121
  905.0 1.4 convolution_bitcast_fusion.7
  906.4 1.4 convolution_bitcast_fusion.6
  907.8 143.1 %all-reduce = (f32[36,36]{1,0:T(8,128)S(1)}, f32[36,36]{1,0:T(8,128)S(1)}) all-reduce(f32[36,36]{1,0:T(8,128)S(1)} %convolution_bitcast_fusion.7, f32[36,36]{1,0:T(8,128)S(1)} %convolution_bitcast_fusion.6), channel_id=1, replica_groups=mesh['row'=32,'col'=8] {'row'}, use_global_device_ids=true, to_apply=%region_55.58 | all-reduce | flops 2592 | bytes 20736 | tf_op jit(solution)/shard_map/psum | solution.py:133
  1052.1 1.4 fusion.490
  1054.4 137.9 %psum.70 = f32[36,36]{0,1:T(8,128)S(1)} all-reduce(f32[36,36]{0,1:T(8,128)S(1)} %convolution_bitcast_fusion.5), channel_id=1, replica_groups=mesh['row'=32,'col'=8] {'row'}, use_global_device_ids=true, to_apply=%region_57.60 | all-reduce | flops 1296 | bytes 10368 | tf_op jit(solution)/shard_map/psum | solution.py:137
  1193.7 6.6 cholesky.42
  1201.6 5.5 custom-call.11
  1210.9 137.7 %psum.71 = f32[2,36,36]{1,2,0:T(8,128)S(1)} all-reduce(f32[2,36,36]{1,2,0:T(8,128)S(1)} %pad_maximum_fusion.24), channel_id=1, replica_groups=mesh['row'=32,'col'=8] {'row'}, use_global_device_ids=true, to_apply=%region_60.63 | all-reduce | flops 2592 | bytes 20736 | tf_op jit(solution)/shard_map/psum | solution.py:158
  (172 shorter events, 86.0 us)
Async XLA Ops:
  7.2 234.8 %all-gather.3.cloned.1.call-start = ((), (), s32[]{:S(2)}) async-start(), calls=%async_computation | async-start | bytes 5406720 | tf_op jit(solution)/shard_map/all_gather | solution.py:102
  156.2 4.1 copy-start.15
  162.7 227.0 %all-reduce.4.cloned.1.call-start = ((), (), s32[]{:S(2)}) async-start(), calls=%async_computation.1 | async-start | bytes 655360 | tf_op jit(solution)/shard_map/psum | solution.py:121
  172.2 4.4 copy-start.3
  178.0 79.9 %copy-start = (bf16[2,1024,128]{2,1,0:T(8,128)(2,1)}, bf16[2,1024,128]{2,1,0:T(8,128)(2,1)S(1)}, u32[]{:S(2)}) copy-start(bf16[2,1024,128]{2,1,0:T(8,128)(2,1)S(1)} %get-tuple-element.571) | copy-start | bytes 1572868
  262.8 4.9 copy-start.10
  272.5 14.4 %copy-start.6 = (f32[2,36,1024]{2,1,0:T(8,128)S(1)}, f32[2,36,1024]{2,1,0:T(8,128)}, u32[]{:S(2)}) copy-start(f32[2,36,1024]{2,1,0:T(8,128)} %get-tuple-element.623) | copy-start | bytes 884740
  277.3 112.4 %copy-start.19 = (f32[1024]{0:T(1024)S(1)}, f32[1024]{0:T(1024)}, u32[]{:S(2)}) copy-start(f32[1024]{0:T(1024)} %param.60) | copy-start | bytes 12292
  290.0 471.1 %all-gather.5.cloned.1.call-start = ((), (), s32[]{:S(2)}) async-start(), calls=%async_computation.2 | async-start | bytes 5406720 | tf_op jit(solution)/shard_map/all_gather | solution.py:102
  534.2 226.9 %copy-start.13 = (f32[36,36]{1,0:T(8,128)}, f32[36,36]{1,0:T(8,128)S(1)}, u32[]{:S(2)}) copy-start(f32[36,36]{1,0:T(8,128)S(1)} %psum.65) | copy-start | bytes 15556
  535.6 0.7 copy-start.2
  678.1 4.1 copy-start.17
  684.5 220.5 %all-reduce.6.cloned.1.call-start = ((), (), s32[]{:S(2)}) async-start(), calls=%async_computation.3 | async-start | bytes 655360 | tf_op jit(solution)/shard_map/psum | solution.py:121
  761.1 2.3 copy-start.1
  785.4 0.7 copy-start.11
  790.8 13.1 copy-start.7
  790.8 13.1 copy-start.8
  790.8 13.1 copy-start.9
  795.7 8.2 copy-start.12
  795.7 10.8 copy-start.14
  795.7 10.8 copy-start.16
  803.9 388.4 %copy-start.18 = (f32[36,36]{1,0:T(8,128)S(1)}, f32[36,36]{1,0:T(8,128)}, u32[]{:S(2)}) copy-start(f32[36,36]{1,0:T(8,128)} %copy-done.17) | copy-start | bytes 15556
  803.9 389.2 %copy-start.20 = (f32[36,36]{1,0:T(8,128)S(1)}, f32[36,36]{1,0:T(8,128)}, u32[]{:S(2)}) copy-start(f32[36,36]{1,0:T(8,128)} %convolution_add_fusion.36) | copy-start | bytes 15556
  806.5 403.3 %copy-start.5 = (f32[1,36,1024]{2,0,1:T(1,128)S(1)}, f32[1,36,1024]{2,0,1:T(1,128)}, u32[]{:S(2)}) copy-start(f32[1,36,1024]{2,0,1:T(1,128)} %get-tuple-element.587) | copy-start | bytes 442372
  806.5 403.9 %copy-start.4 = (f32[1,36,1024]{2,0,1:T(1,128)S(1)}, f32[1,36,1024]{2,0,1:T(1,128)}, u32[]{:S(2)}) copy-start(f32[1,36,1024]{2,0,1:T(1,128)} %get-tuple-element.586) | copy-start | bytes 442372
Sparse Core Ops, SparseCore 0:
  162.8 79.1 all-gather.2
  290.1 99.5 all-reduce.3
  684.7 76.3 all-gather.4
  806.6 98.3 all-reduce.5
where the time goes:
time: 1360 us
  blocking collectives  844 us (62%)
  waiting for transfers between devices  335 us (25%)
  matrix products  92.1 us (7%)
  other arithmetic  43.3 us (3%)
  between operations  21.8 us (2%)
  local copies, waits for them, and re-layouts  19.4 us (1%)
    psum x2, waiting for transfers between devices, apply_operator(): summed = lax.psum(total, 'col')  197 us
    psum x1, blocking collectives, body(): lax.psum(inner_products(incident, incident), 'row')  144 us
    psum x1, blocking collectives, body(): lax.psum((inner_products(image, basis_one), inner_products(image, basis_t...  143 us
    psum x1, blocking collectives, body(): coupling_one = lax.psum(inner_products(image, basis_one), 'row')  143 us
    psum x1, blocking collectives, body(): gram_two = lax.psum(inner_products(rest, rest), 'row')  138 us
    psum x1, blocking collectives, body(): gram_one = lax.psum(inner_products(rest, rest), 'row')  138 us
    psum x1, blocking collectives, body(): coefficients = lax.psum(project(harmonics, solution), 'row')  138 us
    all_gather x2, waiting for transfers between devices, apply_operator(): gathered = lax.all_gather(rounded, 'row', axis=2, tiled=True)  138 us
  transfers between devices with their start and end apart: 4, of which 4 were waited for; matrix products, arithmetic and copies ran while one was open for 1% of the time, Pallas kernels for 0%

commit v1 on v0

--- a/solution.py
+++ b/solution.py
@@ -5,6 +5,13 @@
 from jax.sharding import PartitionSpec as P
 
 highest = lax.Precision.HIGHEST
+
+
+def swapped_in(x, axis, dim):
+    size = lax.axis_size(axis)
+    parts = jnp.stack([x for _ in range(size)])
+    parts = lax.all_to_all(parts, axis, split_axis=0, concat_axis=0)
+    return jnp.concatenate(parts, axis=dim)
 
 
 def dense_term(vector, block):
@@ -99,7 +106,7 @@
 
     def apply_operator(vector):
         rounded = vector.astype(jnp.bfloat16)
-        gathered = lax.all_gather(rounded, "row", axis=2, tiled=True)
+        gathered = swapped_in(rounded, "row", 2)
         far_pieces = [
             lax.dynamic_slice_in_dim(gathered, (column * blocks + number) * elements, elements, 2)
             for number in range(blocks)

time: 1360 us -> 1560 us (1.15)
  local copies, waits for them, and re-layouts: 19.4 us -> 180 us
    all_gather x2 -> x0, waiting for transfers between devices: 138 us -> none  [apply_operator(): gathered = lax.all_gather(rounded, 'row', axis=2, tiled=True)]
    all_to_all x0 -> x2, waiting for transfers between devices: none -> 117 us  [swapped_in(): parts = lax.all_to_all(parts, axis, split_axis=0, concat_axis=0)]
    another operation x0 -> x18, local copies, waits for them, and re-layouts: none -> 92.3 us
    cond x0 -> x56, local copies, waits for them, and re-layouts: none -> 49.9 us
    psum x2, waiting for transfers between devices: 197 us -> 223 us  [apply_operator(): summed = lax.psum(total, 'col')]
    reshape x0 -> x2, local copies, waits for them, and re-layouts: none -> 19.1 us  [swapped_in(): return jnp.concatenate(parts, axis=dim)]
  transfers between devices with their start and end apart: 4 -> 4, of which waited for: 4 -> 4; matrix products, arithmetic and copies ran while one was open for 1% -> 0% of each run, Pallas kernels for 0% -> 0%
where the time goes in v1:
time: 1560 us; the launch traced here: 1540 us
  blocking collectives  856 us (55%)
  waiting for transfers between devices  340 us (22%)
  local copies, waits for them, and re-layouts  180 us (12%)
  matrix products  80.6 us (5%)
  other arithmetic  40 us (3%)
  between operations  22.6 us (1%)
    psum x2, waiting for transfers between devices, apply_operator(): summed = lax.psum(total, 'col')  223 us
    psum x1, blocking collectives, body(): lax.psum(inner_products(incident, incident), 'row')  148 us
    psum x1, blocking collectives, body(): gram_one = lax.psum(inner_products(rest, rest), 'row')  147 us
    psum x1, blocking collectives, body(): lax.psum((inner_products(image, basis_one), inner_products(image, basis_t...  143 us
    psum x1, blocking collectives, body(): coupling_one = lax.psum(inner_products(image, basis_one), 'row')  143 us
    psum x1, blocking collectives, body(): coefficients = lax.psum(project(harmonics, solution), 'row')  138 us
    psum x1, blocking collectives, body(): gram_two = lax.psum(inner_products(rest, rest), 'row')  138 us
    all_to_all x2, waiting for transfers between devices, swapped_in(): parts = lax.all_to_all(parts, axis, split_axis=0, concat_axis=0)  117 us
  transfers between devices with their start and end apart: 4, of which 4 were waited for; matrix products, arithmetic and copies ran while one was open for 0% of the time, Pallas kernels for 0%

profile of v1, /device:TPU:0, one launch (start us, length us, event | category | flops | bytes accessed | tf_op | source)
XLA Modules:
  0.0 1543.6 jit_solution(16733102701394399664)
XLA Ops:
  8.8 148.0 %psum.63 = f32[36,36]{0,1:T(8,128)S(1)} all-reduce(f32[36,36]{0,1:T(8,128)S(1)} %convolution_bitcast_fusion.7), channel_id=1, replica_groups=mesh['row'=32,'col'=8] {'row'}, use_global_device_ids=true, to_apply=%region_0.0 | all-reduce | flops 1296 | bytes 10368 | tf_op jit(solution)/shard_map/psum | solution.py:131
  156.9 3.3 cholesky.81
  161.6 2.8 custom-call.13
  166.3 6.5 stack.463
  172.8 5.0 all-to-all-start
  190.7 62.2 %all-to-all-done = bf16[32,2,36,1024]{3,1,2,0:T(2,128)(2,1)} async-done(((bf16[32,2,36,1024]{3,1,2,0:T(2,128)(2,1)}), bf16[32,2,36,1024]{3,1,2,0:T(2,128)(2,1)}, u32[]{:S(2)}, u32[]{:S(2)}) %all-to-all-start) | async-done | bytes 4718624 | tf_op jit(solution)/shard_map/all_to_all | solution.py:13
  252.9 9.6 copy.253
  262.4 12.6 conditional.31
  262.6 4.9 copy.131
  267.6 2.3 copy-done.25
  275.0 12.4 conditional.30
  275.0 4.9 copy.129
  280.0 2.3 copy-done.26
  287.5 12.5 conditional.29
  287.5 4.9 copy.127
  300.0 12.6 conditional.27
  300.2 4.9 copy.123
  305.1 2.3 copy-done.28
  312.6 12.4 conditional.26
  312.6 4.9 copy.121
  325.1 13.1 conditional.24
  325.1 5.0 copy.117
  330.1 2.3 copy-done.30
  338.1 13.5 conditional.25
  338.5 5.0 copy.118
  351.6 12.4 conditional.28
  351.6 4.9 copy.125
  366.6 6.6 conditional.35
  373.3 3.0 add_add_fusion.1
  376.3 121.2 %all-reduce.4.cloned.1.call-done = f32[2,36,1024]{2,0,1:T(2,128)} async-done(((f32[2,36,1024]{2,0,1:T(2,128)}), f32[2,36,1024]{2,0,1:T(2,128)}) %all-reduce.4.cloned.1.call-update) | async-done | bytes 294928 | tf_op jit(solution)/shard_map/psum | solution.py:128
  499.9 143.1 %psum.65 = f32[36,36]{1,0:T(8,128)S(1)} all-reduce(f32[36,36]{1,0:T(8,128)S(1)} %convolution_bitcast_fusion.5), channel_id=1, replica_groups=mesh['row'=32,'col'=8] {'row'}, use_global_device_ids=true, to_apply=%region_28.31 | all-reduce | flops 1296 | bytes 10368 | tf_op jit(solution)/shard_map/psum | solution.py:134
  646.0 146.8 %psum.66 = f32[36,36]{1,0:T(8,128)S(1)} all-reduce(f32[36,36]{1,0:T(8,128)S(1)} %convolution_bitcast_fusion.4), channel_id=1, replica_groups=mesh['row'=32,'col'=8] {'row'}, use_global_device_ids=true, to_apply=%region_29.32 | all-reduce | flops 1296 | bytes 10368 | tf_op jit(solution)/shard_map/psum | solution.py:136
  792.9 3.3 cholesky.92
  797.5 3.4 custom-call.14
  804.4 6.5 stack.464
  810.9 4.9 all-to-all-start.1
  818.6 54.5 %all-to-all-done.1 = bf16[32,2,36,1024]{3,1,2,0:T(2,128)(2,1)} async-done(((bf16[32,2,36,1024]{3,1,2,0:T(2,128)(2,1)}), bf16[32,2,36,1024]{3,1,2,0:T(2,128)(2,1)}, u32[]{:S(2)}, u32[]{:S(2)}) %all-to-all-start.1) | async-done | bytes 4718624 | tf_op jit(solution)/shard_map/all_to_all | solution.py:13
  873.1 9.6 copy.254
  882.6 13.5 conditional.37
  883.0 5.0 copy.153
  888.1 2.3 copy-done.33
  896.1 13.1 conditional.36
  896.1 5.0 copy.152
  909.2 12.5 conditional.38
  909.2 5.0 copy.156
  921.6 11.0 conditional.39
  921.8 5.0 copy.158
  932.7 10.9 conditional.40
  932.7 5.0 copy.160
  943.6 10.9 conditional.41
  943.6 5.0 copy.162
  954.5 11.1 conditional.42
  954.7 5.0 copy.164
  966.6 11.6 conditional.43
  966.6 5.0 copy.166
  971.6 2.3 copy-done.40
  982.8 5.0 conditional.47
  987.8 2.4 add_add_fusion
  991.1 102.3 %all-reduce.6.cloned.1.call-done = f32[2,36,1024]{2,0,1:T(2,128)} async-done(((f32[2,36,1024]{2,0,1:T(2,128)}), f32[2,36,1024]{2,0,1:T(2,128)}) %all-reduce.6.cloned.1.call-update) | async-done | bytes 294928 | tf_op jit(solution)/shard_map/psum | solution.py:128
  1095.5 143.1 %all-reduce = (f32[36,36]{1,0:T(8,128)S(1)}, f32[36,36]{1,0:T(8,128)S(1)}) all-reduce(f32[36,36]{1,0:T(8,128)S(1)} %convolution_bitcast_fusion.1, f32[36,36]{1,0:T(8,128)S(1)} %convolution_bitcast_fusion.2), channel_id=1, replica_groups=mesh['row'=32,'col'=8] {'row'}, use_global_device_ids=true, to_apply=%region_56.59 | all-reduce | flops 2592 | bytes 20736 | tf_op jit(solution)/shard_map/psum | solution.py:140
  1242.8 137.7 %psum.70 = f32[36,36]{0,1:T(8,128)S(1)} all-reduce(f32[36,36]{0,1:T(8,128)S(1)} %convolution_bitcast_fusion), channel_id=1, replica_groups=mesh['row'=32,'col'=8] {'row'}, use_global_device_ids=true, to_apply=%region_57.60 | all-reduce | flops 1296 | bytes 10368 | tf_op jit(solution)/shard_map/psum | solution.py:144
  1380.9 6.6 cholesky.42
  1388.8 5.5 custom-call.11
  1398.2 137.7 %psum.71 = f32[2,36,36]{1,2,0:T(8,128)S(1)} all-reduce(f32[2,36,36]{1,2,0:T(8,128)S(1)} %pad_maximum_fusion.24), channel_id=1, replica_groups=mesh['row'=32,'col'=8] {'row'}, use_global_device_ids=true, to_apply=%region_60.63 | all-reduce | flops 2592 | bytes 20736 | tf_op jit(solution)/shard_map/psum | solution.py:165
  (264 shorter events, 147.1 us)
Async XLA Ops:
  172.8 5.3 copy-start.56
  172.8 13.6 copy-start.58
  172.8 14.3 copy-start.51
  172.8 14.3 copy-start.52
  172.8 80.1 %all-to-all-start = ((bf16[32,2,36,1024]{3,1,2,0:T(2,128)(2,1)}), bf16[32,2,36,1024]{3,1,2,0:T(2,128)(2,1)}, u32[]{:S(2)}, u32[]{:S(2)}) async-start(bf16[32,2,36,1024]{3,1,2,0:T(2,128)(2,1)} %stack.463), calls=%async_computation | async-start | bytes 9437184 | tf_op jit(solution)/shard_map/all_to_all | solution.py:13
  177.8 319.7 %all-reduce.4.cloned.1.call-start = ((), (), s32[]{:S(2)}) async-start(), calls=%async_computation.2 | async-start | bytes 589824 | tf_op jit(solution)/shard_map/psum | solution.py:128
  186.4 2.9 copy-start.41
  267.5 2.4 copy-start.25
  280.0 2.4 copy-start.26
  292.5 2.4 copy-start.27
  305.1 2.4 copy-start.28
  317.6 2.4 copy-start.29
  325.1 7.4 copy-start
  330.1 2.4 copy-start.30
  338.5 7.4 copy-start.2
  343.6 2.4 copy-start.31
  356.6 2.4 copy-start.32
  364.1 0.7 copy-start.46
  365.1 0.7 copy-start.47
  365.9 0.7 copy-start.48
  365.9 131.6 %copy-start.57 = (f32[1024]{0:T(1024)S(1)}, f32[1024]{0:T(1024)}, u32[]{:S(2)}) copy-start(f32[1024]{0:T(1024)} %param.60) | copy-start | bytes 12292
  498.6 0.7 copy-start.43
  644.8 0.7 copy-start.42
  796.2 14.6 copy-start.53
  810.9 62.2 %all-to-all-start.1 = ((bf16[32,2,36,1024]{3,1,2,0:T(2,128)(2,1)}), bf16[32,2,36,1024]{3,1,2,0:T(2,128)(2,1)}, u32[]{:S(2)}, u32[]{:S(2)}) async-start(bf16[32,2,36,1024]{3,1,2,0:T(2,128)(2,1)} %stack.464), calls=%async_computation.1 | async-start | bytes 9437184 | tf_op jit(solution)/shard_map/all_to_all | solution.py:13
  815.7 277.6 %all-reduce.6.cloned.1.call-start = ((), (), s32[]{:S(2)}) async-start(), calls=%async_computation.3 | async-start | bytes 589824 | tf_op jit(solution)/shard_map/psum | solution.py:128
  883.0 7.4 copy-start.3
  888.0 2.4 copy-start.33
  896.1 7.4 copy-start.1
  901.1 2.4 copy-start.34
  914.1 2.4 copy-start.35
  926.7 2.4 copy-start.36
  937.6 2.4 copy-start.37
  948.5 2.4 copy-start.38
  959.6 2.4 copy-start.39
  965.6 1.0 copy-start.8
  965.6 1.0 copy-start.15
  971.6 2.4 copy-start.40
  978.2 0.9 copy-start.7
  978.2 1.0 copy-start.13
  979.3 0.7 copy-start.49
  979.3 1.1 copy-start.6
  979.3 1.1 copy-start.11
  980.9 1.0 copy-start.5
  980.9 1.0 copy-start.9
  982.8 5.0 copy-start.50
  982.8 110.6 %copy-start.4 = (f32[2,36,1024]{2,0,1:T(2,128)S(1)}, f32[2,36,1024]{2,0,1:T(2,128)}, u32[]{:S(2)}) copy-start(f32[2,36,1024]{2,0,1:T(2,128)} %get-tuple-element.863) | copy-start | bytes 884740
  987.8 253.1 %copy-start.54 = (f32[36,36]{1,0:T(8,128)S(1)}, f32[36,36]{1,0:T(8,128)}, u32[]{:S(2)}) copy-start(f32[36,36]{1,0:T(8,128)} %copy-done.53) | copy-start | bytes 15556
  987.8 253.9 %copy-start.55 = (f32[36,36]{1,0:T(8,128)S(1)}, f32[36,36]{1,0:T(8,128)}, u32[]{:S(2)}) copy-start(f32[36,36]{1,0:T(8,128)} %convolution_add_fusion.36) | copy-start | bytes 15556
  987.8 408.3 %copy-start.45 = (f32[1,36,1024]{2,0,1:T(1,128)S(1)}, f32[1,36,1024]{2,0,1:T(1,128)}, u32[]{:S(2)}) copy-start(f32[1,36,1024]{2,0,1:T(1,128)} %get-tuple-element.883) | copy-start | bytes 442372
  990.2 407.4 %copy-start.44 = (f32[1,36,1024]{2,0,1:T(1,128)S(1)}, f32[1,36,1024]{2,0,1:T(1,128)}, u32[]{:S(2)}) copy-start(f32[1,36,1024]{2,0,1:T(1,128)} %get-tuple-element.882) | copy-start | bytes 442372
Sparse Core Ops, SparseCore 0:
  376.4 121.0 all-reduce.3
  990.4 102.9 all-reduce.5
